TPU v7x, 32 devices: a whole 2x2x4 slice. The times are simulated.
32 devices in a mesh: group: 1, seq: 32 (over z, y, x, core).
Axes of the slice: x: 2, y: 2, z: 4, core: 2. Of those that a mesh axis runs over, the one named last changes fastest.
Arguments:
- enc_x: bfloat16 [256, 1280], P(('group', 'seq')), may hold values from -1.5 to 1.5
- enc_qkv: bfloat16 [256, 3, 640], P(('group', 'seq'))
- w_eo: bfloat16 [640, 1280], replicated, may hold values from -0.25 to 0.25
- w_kv: bfloat16 [1280, 2048], replicated, may hold values from -0.15625 to 0.15625
- dec_x: bfloat16 [32, 8192], P(('group', 'seq')), may hold values from -1.5 to 1.5
- w_q: bfloat16 [8192, 8192], P(None, 'seq'), may hold values from -0.0625 to 0.0625
- w_o: bfloat16 [8192, 8192], P(None, 'seq'), may hold values from -0.0625 to 0.0625
- cache_kv: bfloat16 [32, 4, 128, 2048], P(('group', 'seq'))
- doc_tile: int32 [32], P(('group', 'seq')), may hold values from 0 to 1
- cached_count: int32 [32], P(('group', 'seq')), may hold values from 0 to 3
Outputs:
- dec_out: bfloat16 [32, 8192], P(('group', 'seq'))
All inputs are finite; a program needn't handle non-finite values.
Results may differ from a plain program's by a relative error of at most 0.017.
The roundings to bfloat16 on the way count: a program that leaves them out, or rounds other values in their place, can miss the bound.
Values may be sent and summed in bfloat16 or wider, within the bound.
A program may use at most 64 MiB of HBM per device.

v0:
```python
import jax
import jax.numpy as jnp
from jax import lax
from jax.sharding import PartitionSpec as P

EH = 8
EHD = 80
HD = 128
TILE_LEN = 128


def layer_norm(values):
    center = values - jnp.mean(values, axis=-1, keepdims=True)
    spread = jnp.mean(center * center, axis=-1, keepdims=True)
    return center * lax.rsqrt(spread + 1e-05)


def doc_attend(query_row, doc_kv, filled):
    length = doc_kv.shape[0]
    width = doc_kv.shape[1] // 2
    kv_heads = width // HD
    query_heads = query_row.reshape(kv_heads, -1, HD)
    key_heads = doc_kv[:, :width].reshape(length, kv_heads, HD)
    value_heads = doc_kv[:, width:].reshape(length, kv_heads, HD)
    scores = jnp.einsum(
        "gqd,kgd->gqk", query_heads, key_heads, preferred_element_type=jnp.float32
    ) * HD ** (-0.5)
    inside = jnp.arange(length, dtype=jnp.int32) // TILE_LEN <= filled
    scores = jnp.where(inside[None, None, :], scores, -jnp.inf)
    weights = jax.nn.softmax(scores, axis=-1).astype(jnp.bfloat16)
    result = jnp.einsum("gqk,kgd->gqd", weights, value_heads, preferred_element_type=jnp.float32)
    return result.reshape(1, -1).astype(jnp.bfloat16)


def local(enc_x, enc_qkv, w_eo, w_kv, dec_x, w_q, w_o, cache_kv, doc_tile, cached_count):
    tok_rows = enc_x.shape[0]
    query_heads = enc_qkv[:, 0].reshape(tok_rows, EH, EHD)
    key_piece = lax.all_gather(enc_qkv[:, 1], "seq", axis=0, tiled=True)
    value_piece = lax.all_gather(enc_qkv[:, 2], "seq", axis=0, tiled=True)
    length = key_piece.shape[0]
    key_heads = key_piece.reshape(length, EH, EHD)
    value_heads = value_piece.reshape(length, EH, EHD)
    scores = jnp.einsum(
        "qhd,khd->hqk", query_heads, key_heads, preferred_element_type=jnp.float32
    ) * EHD ** (-0.5)
    old_max = jnp.full((EH, tok_rows), -1e30, jnp.float32)
    new_max = jnp.maximum(old_max, jnp.max(scores, axis=-1))
    powers = jnp.exp(scores - new_max[:, :, None])
    new_total = jnp.sum(powers, axis=-1)
    new_acc = jnp.einsum(
        "hqk,khd->hqd", powers.astype(jnp.bfloat16), value_heads, preferred_element_type=jnp.float32
    )
    enc_attn = (
        (new_acc / new_total[:, :, None])
        .transpose(1, 0, 2)
        .reshape(tok_rows, -1)
        .astype(jnp.bfloat16)
    )
    resid = enc_x.astype(jnp.float32) + jnp.dot(enc_attn, w_eo, preferred_element_type=jnp.float32)
    features = layer_norm(resid).astype(jnp.bfloat16)
    tile_start = doc_tile[0] * TILE_LEN
    x_float = dec_x.astype(jnp.float32)
    normed = (
        x_float * lax.rsqrt(jnp.mean(x_float * x_float, axis=-1, keepdims=True) + 1e-05)
    ).astype(jnp.bfloat16)
    query_cols = jnp.dot(
        lax.all_gather(normed, "seq", axis=0, tiled=True), w_q, preferred_element_type=jnp.float32
    ).astype(jnp.bfloat16)
    query_row = lax.all_to_all(query_cols, "seq", split_axis=0, concat_axis=1, tiled=True)
    zero = jnp.zeros((), jnp.int32)
    filled = cached_count[0]
    local_kv = jnp.dot(features, w_kv, preferred_element_type=jnp.float32).astype(jnp.bfloat16)
    buffer = jnp.zeros((TILE_LEN, w_kv.shape[1]), jnp.bfloat16)
    piece = lax.all_gather(local_kv, "seq", axis=0, tiled=True)
    length = piece.shape[0]
    position = jnp.arange(length, dtype=jnp.int32) - tile_start
    inside = (position >= 0) & (position < buffer.shape[0])
    clipped = jnp.clip(position, 0, buffer.shape[0] - 1)
    tile_kv = buffer.at[clipped].add(jnp.where(inside[:, None], piece, jnp.zeros_like(piece)))
    doc_kv = lax.dynamic_update_slice(cache_kv[0], tile_kv[None], (filled, zero, zero))
    doc_kv = doc_kv.reshape(-1, doc_kv.shape[-1])
    dec_attn = doc_attend(query_row[0], doc_kv, filled)
    output_cols = jnp.dot(
        lax.all_gather(dec_attn, "seq", axis=0, tiled=True), w_o, preferred_element_type=jnp.float32
    ).astype(jnp.bfloat16)
    attn_out = lax.all_to_all(output_cols, "seq", split_axis=0, concat_axis=1, tiled=True)
    return (x_float + attn_out.astype(jnp.float32)).astype(jnp.bfloat16)


def solution(mesh):
    return jax.shard_map(
        local,
        mesh=mesh,
        in_specs=(
            P(("group", "seq"), None),
            P(("group", "seq"), None, None),
            P(),
            P(),
            P(("group", "seq"), None),
            P(None, "seq"),
            P(None, "seq"),
            P(("group", "seq"), None, None, None),
            P(("group", "seq")),
            P(("group", "seq")),
        ),
        out_specs=P(("group", "seq"), None),
        check_vma=False,
    )
```

profile of v0, /device:TPU:0, one launch (start us, length us, event | category | flops | bytes accessed | tf_op | source)
XLA Modules:
  0.0 227.0 jit_solution(8860197279776940830)
XLA Ops:
  6.5 3.3 %copy.64 = bf16[1,4,128,2048]{3,2,1,0:T(8,128)(2,1)} copy(bf16[1,4,128,2048]{3,2,1,0:T(8,128)(2,1)} %param.17) | data formatting | bytes 4194304
  9.9 44.1 %all-gather = bf16[256,1,640]{2,0,1:T(8,128)(2,1)S(1)} all-gather(bf16[8,1,640]{2,0,1:T(8,128)(2,1)S(1)} %get-tuple-element.9), channel_id=2, replica_groups=mesh['group'=1,'seq'=32] {'seq'}, dimensions={0}, use_global_device_ids=true | all-gather | bytes 337920 | tf_op jit(solution)/shard_map/all_gather | solution.py:38
  54.0 0.2 copy.31
  54.3 0.2 fusion.32
  54.5 37.5 %all-gather.1 = bf16[256,1,640]{2,0,1:T(8,128)(2,1)S(1)} all-gather(bf16[8,1,640]{2,0,1:T(8,128)(2,1)S(1)} %get-tuple-element.8), channel_id=3, replica_groups=mesh['group'=1,'seq'=32] {'seq'}, dimensions={0}, use_global_device_ids=true | all-gather | bytes 337920 | tf_op jit(solution)/shard_map/all_gather | solution.py:39
  92.0 0.2 copy.33
  92.2 0.2 fusion.18
  92.3 0.2 fusion.5
  92.7 0.4 fusion.33
  93.2 0.2 multiply_reduce_fusion
  93.4 3.9 %convolution_convert_fusion = bf16[8,2048]{1,0:T(8,128)(2,1)} fusion(bf16[1280,2048]{1,0:T(8,128)(2,1)} %param.13, f32[8,1280]{1,0:T(8,128)S(1)} %get-tuple-element.13, f32[8]{0:T(128)S(1)} %add_rsqrt_fusion, f32[8]{0:T(128)S(1)} %broadcast_multiply_fusion), kind=kOutput, calls=%fused_computation.3 | convolution fusion | flops 41990144 | bytes 5316672 | tf_op jit(solution)/shard_map/dot_general | solution.py:72
  97.4 0.6 multiply_reduce_fusion.1
  98.6 41.1 %all-gather.2 = bf16[32,1,8192]{2,1,0:T(2,128)(2,1)S(1)} all-gather(bf16[1,1,8192]{2,1,0:T(2,128)(2,1)S(1)} %convert_bitcast_fusion), channel_id=1, replica_groups=mesh['group'=1,'seq'=32] {'seq'}, dimensions={0}, use_global_device_ids=true | all-gather | bytes 540672 | tf_op jit(solution)/shard_map/all_gather | solution.py:67
  139.7 3.2 %fusion.6 = bf16[32,1,256]{2,0,1:T(8,128)(2,1)S(1)} fusion(bf16[8192,256]{1,0:T(8,128)(2,1)} %param.15, bf16[32,1,8192]{2,1,0:T(2,128)(2,1)S(1)} %all-gather.2), kind=kOutput, calls=%fused_computation.15 | convolution fusion | flops 134225920 | bytes 4734976 | tf_op jit(solution)/shard_map/dot_general | solution.py:66
  142.9 0.5 broadcast.127
  143.5 0.6 reduce.2
  144.1 0.6 reshape.152
  144.7 2.5 %all-to-all-start = ((bf16[32,2,128]{2,1,0:T(2,128)(2,1)}), bf16[32,2,128]{2,1,0:T(2,128)(2,1)S(1)}, u32[]{:S(2)}, u32[]{:S(2)}) async-start(bf16[32,2,128]{2,1,0:T(2,128)(2,1)} %reshape.152), calls=%async_computation | async-start | bytes 32768 | tf_op jit(solution)/shard_map/all_to_all | solution.py:69
  148.5 5.8 %all-to-all-done = bf16[32,2,128]{2,1,0:T(2,128)(2,1)S(1)} async-done(((bf16[32,2,128]{2,1,0:T(2,128)(2,1)}), bf16[32,2,128]{2,1,0:T(2,128)(2,1)S(1)}, u32[]{:S(2)}, u32[]{:S(2)}) %all-to-all-start) | async-done | bytes 16416 | tf_op jit(solution)/shard_map/all_to_all | solution.py:69
  154.5 4.8 %scatter_custom_fusion = bf16[128,2048]{1,0:T(8,128)(2,1)S(1)} fusion(s32[256]{0:T(256)S(1)} %bitcast.58, bf16[256,2048]{1,0:T(8,128)(2,1)} %all-gather.6.cloned.1.call-done, pred[256]{0:T(512)(128)(4,1)S(1)} %compare_and_fusion, bf16[]{:T(256)} %constant.44.clone.1), kind=kCustom, calls=%fused_computation.17 | custom fusion | flops 1048576 | bytes 1574400 | tf_op jit(solution)/shard_map/scatter-add | solution.py:79
  159.3 0.8 bitcast_dynamic-update-slice_fusion
  160.1 3.0 %fusion.30 = (bf16[512,1024]{1,0:T(8,128)(2,1)}, bf16[512,1024]{1,0:T(8,128)(2,1)}) fusion(bf16[512,2048]{1,0:T(8,128)(2,1)} %bitcast.51), kind=kLoop, calls=%fused_computation.55 | loop fusion | bytes 4194304 | tf_op jit(solution)/shard_map/slice | solution.py:23
  163.1 1.5 copy.44
  164.6 0.2 fusion.3
  164.9 0.2 fusion.34
  165.1 1.5 copy.45
  166.6 0.4 convolution_convert_fusion.2
  167.0 39.7 %all-gather.3 = bf16[32,1,8192]{2,1,0:T(2,128)(2,1)S(1)} all-gather(bf16[1,1,8192]{2,1,0:T(2,128)(2,1)S(1)} %reshape.146), channel_id=1, replica_groups=mesh['group'=1,'seq'=32] {'seq'}, dimensions={0}, use_global_device_ids=true | all-gather | bytes 540672 | tf_op jit(solution)/shard_map/all_gather | solution.py:84
  206.7 3.1 %fusion.7 = bf16[32,1,256]{2,0,1:T(8,128)(2,1)S(1)} fusion(bf16[8192,256]{1,0:T(8,128)(2,1)} %param.16, bf16[32,1,8192]{2,1,0:T(2,128)(2,1)S(1)} %all-gather.3), kind=kOutput, calls=%fused_computation.16 | convolution fusion | flops 134225920 | bytes 4734976 | tf_op jit(solution)/shard_map/dot_general | solution.py:83
  209.9 0.6 reduce.3
  210.6 8.9 %all_to_all.26 = bf16[32,2,128]{2,1,0:T(2,128)(2,1)S(1)} all-to-all(bf16[32,2,128]{2,1,0:T(2,128)(2,1)S(1)} %reshape.154), channel_id=1, replica_groups=mesh['group'=1,'seq'=32] {'seq'}, dimensions={0} | all-to-all | bytes 32768 | tf_op jit(solution)/shard_map/all_to_all | solution.py:86
  219.4 0.7 fusion.21
  (28 shorter events, 0.5 us)
Async XLA Ops:
  6.5 86.2 %copy-start = (bf16[640,1280]{1,0:T(8,128)(2,1)S(1)}, bf16[640,1280]{1,0:T(8,128)(2,1)}, u32[]{:S(2)}) copy-start(bf16[640,1280]{1,0:T(8,128)(2,1)} %param.12) | copy-start | bytes 4915204
  6.5 86.2 %copy-start.3 = (bf16[8,1280]{1,0:T(8,128)(2,1)S(1)}, bf16[8,1280]{1,0:T(8,128)(2,1)}, u32[]{:S(2)}) copy-start(bf16[8,1280]{1,0:T(8,128)(2,1)} %param.10) | copy-start | bytes 61444
  6.5 3.3 %copy-start.2 = (bf16[8,3,640]{2,0,1:T(8,128)(2,1)S(1)}, bf16[8,3,640]{2,0,1:T(8,128)(2,1)}, u32[]{:S(2)}) copy-start(bf16[8,3,640]{2,0,1:T(8,128)(2,1)} %param.11) | copy-start | bytes 92164
  6.5 147.9 %all-gather.6.cloned.1.call-start = ((), (), s32[]{:S(2)}) async-start(), calls=%async_computation.2 | async-start | bytes 1081344 | tf_op jit(solution)/shard_map/all_gather | solution.py:74
  92.0 5.4 %copy-start.1 = (bf16[1,8192]{1,0:T(2,128)(2,1)S(1)}, bf16[1,8192]{1,0:T(2,128)(2,1)}, u32[]{:S(2)}) copy-start(bf16[1,8192]{1,0:T(2,128)(2,1)} %param.14) | copy-start | bytes 49156
  144.7 9.6 %all-to-all-start = ((bf16[32,2,128]{2,1,0:T(2,128)(2,1)}), bf16[32,2,128]{2,1,0:T(2,128)(2,1)S(1)}, u32[]{:S(2)}, u32[]{:S(2)}) async-start(bf16[32,2,128]{2,1,0:T(2,128)(2,1)} %reshape.152), calls=%async_computation | async-start | bytes 32768 | tf_op jit(solution)/shard_map/all_to_all | solution.py:69
Sparse Core Ops, SparseCore 0:
  97.5 51.7 all-gather.5
where the time goes:
time: 227 us
  blocking collectives  171 us (75%)
  between operations  15.5 us (7%)
  local copies, waits for them, and re-layouts  11.9 us (5%)
  matrix products  11.8 us (5%)
  other arithmetic  8.08 us (4%)
  waiting for transfers between devices  5.86 us (3%)
  starting transfers between devices  2.46 us (1%)
    all_gather x1, blocking collectives, local(): key_piece = lax.all_gather(enc_qkv[:, 1], 'seq', axis=0, tiled=True)  44.1 us
    all_gather x1, blocking collectives, local(): lax.all_gather(normed, 'seq', axis=0, tiled=True)  41.1 us
    all_gather x1, blocking collectives, local(): lax.all_gather(dec_attn, 'seq', axis=0, tiled=True)  39.7 us
    all_gather x1, blocking collectives, local(): value_piece = lax.all_gather(enc_qkv[:, 2], 'seq', axis=0, tiled=True)  37.5 us
    all_to_all x1, blocking collectives, local(): lax.all_to_all(output_cols, 'seq', split_axis=0, concat_axis=1, tiled=True)  8.87 us
    unnamed x16, local copies, waits for them, and re-layouts  6.99 us
    all_to_all x1, waiting for transfers between devices, local(): lax.all_to_all(query_cols, 'seq', split_axis=0, concat_axis=1, tiled=True)  5.83 us
    scatter-add x1, other arithmetic, local(): buffer.at[clipped]  4.8 us
  transfers between devices with their start and end apart: 2, of which 1 were waited for; matrix products, arithmetic and copies ran while one was open for 3% of the time, Pallas kernels for 0%

commit v1 on v0

--- a/solution.py
+++ b/solution.py
@@ -1,12 +1,17 @@
+import functools
+
 import jax
 import jax.numpy as jnp
 from jax import lax
+from jax.experimental import pallas as pl
+from jax.experimental.pallas import tpu as pltpu
 from jax.sharding import PartitionSpec as P
 
 EH = 8
 EHD = 80
 HD = 128
 TILE_LEN = 128
+MESH = pl.DeviceIdType.MESH
 
 
 def layer_norm(values):
@@ -87,9 +92,309 @@
     return (x_float + attn_out.astype(jnp.float32)).astype(jnp.bfloat16)
 
 
+def fused_kernel(
+    n, enc_ref, x_ref, tile_ref, count_ref, weo_hbm, wkv_hbm, wq_hbm, wo_hbm, cache_hbm, out_ref,
+    weo, wkv, wq, wo, cache, load_sem,
+    enc_all, enc_send, enc_recv, enc_rows, enc_feat, new_kv,
+    norm_own, norm_all, norm_send, norm_recv,
+    attn_heads, attn_own, attn_all, attn_send, attn_recv,
+    wide, lhs, head_rows,
+    q_out, q_in, q_send, q_recv,
+    o_out, o_in, o_send, o_recv,
+):
+    me = lax.axis_index("seq")
+    inner = 4
+    outer = n // (2 * inner)
+    zi, qi, ci = me // (2 * inner), (me // 2) % inner, me % 2
+
+    def at(kz, kq, kc):
+        return (zi + kz) % outer * (2 * inner) + (qi + kq) % inner * 2 + (ci + kc) % 2
+
+    loads = [
+        pltpu.make_async_copy(src, dst, load_sem.at[i])
+        for i, (src, dst) in enumerate(
+            ((wq_hbm, wq), (weo_hbm, weo), (wkv_hbm, wkv), (cache_hbm, cache), (wo_hbm, wo))
+        )
+    ]
+    for load in loads:
+        load.start()
+
+    barrier = pltpu.get_barrier_semaphore()
+
+    def greet(k, carry):
+        pl.semaphore_signal(barrier, inc=1, device_id={"seq": (me + k) % n}, device_id_type=MESH)
+        return carry
+
+    lax.fori_loop(1, n, greet, 0)
+
+    x_float = x_ref[...].astype(jnp.float32)
+    squares = jnp.sum(jnp.sum(x_float * x_float, axis=1, keepdims=True), axis=0, keepdims=True)
+    normed = (x_float * lax.rsqrt(squares / x_float.size + 1e-05)).astype(jnp.bfloat16)
+    norm_own[...] = normed
+    norm_all[me] = normed
+    enc_all[me] = enc_ref[...]
+    q_out[...] = jnp.zeros_like(q_out)
+    o_out[...] = jnp.zeros_like(o_out)
+    pl.semaphore_wait(barrier, n - 1)
+
+    def gather(own, every, send, recv):
+        def push(src, slot, sem, device):
+            pltpu.make_async_remote_copy(
+                src_ref=src, dst_ref=every.at[slot], send_sem=send.at[sem], recv_sem=recv.at[slot],
+                device_id={"seq": device}, device_id_type=MESH,
+            ).start()
+
+        def take(slot):
+            pltpu.make_async_remote_copy(
+                src_ref=own, dst_ref=every.at[slot], send_sem=send.at[0], recv_sem=recv.at[slot],
+                device_id={"seq": at(0, 0, 1)}, device_id_type=MESH,
+            ).wait_recv()
+
+        def first():
+            for kz in range(1, outer):
+                push(own, me, kz - 1, at(kz, 0, 0))
+            for kq in range(1, inner):
+                push(own, me, outer - 1 + kq - 1, at(0, kq, 0))
+            push(own, me, outer - 1 + inner - 1, at(0, 0, 1))
+
+        def second():
+            for kz in range(1, outer):
+                slot = at(-kz + outer, 0, 0)
+                take(slot)
+                base = outer - 1 + inner * kz
+                for kq in range(1, inner):
+                    push(every.at[slot], slot, base + kq - 1, at(0, kq, 0))
+                push(every.at[slot], slot, base + inner - 1, at(0, 0, 1))
+
+        def third():
+            base = outer - 1 + inner * outer
+            for kz in range(outer):
+                for kq in range(1, inner):
+                    slot = at(-kz + outer, -kq + inner, 0)
+                    take(slot)
+                    push(every.at[slot], slot, base + kz * (inner - 1) + kq - 1, at(0, 0, 1))
+
+        def last():
+            for kz in range(outer):
+                for kq in range(inner):
+                    take(at(-kz + outer, -kq + inner, 1))
+
+        def drain():
+            def one(k, carry):
+                pltpu.make_async_remote_copy(
+                    src_ref=own, dst_ref=every.at[0], send_sem=send.at[k], recv_sem=recv.at[0],
+                    device_id={"seq": at(0, 0, 1)}, device_id_type=MESH,
+                ).wait_send()
+                return carry
+
+            lax.fori_loop(0, n - 1, one, 0)
+
+        return first, second, third, last, drain
+
+    def rows_of(ref, index):
+        return ref.at[pl.ds(pl.multiple_of(index * 8, 8), 8), :]
+
+    def scatter(values, out, into, send, recv):
+        rounded = values.astype(jnp.bfloat16).astype(jnp.float32)
+        out[pl.ds(0, n, stride=8), :] = rounded[:, :HD]
+        out[pl.ds(1, n, stride=8), :] = rounded[:, HD:]
+
+        def one(k, carry):
+            device = (me + k) % n
+            pltpu.make_async_remote_copy(
+                src_ref=rows_of(out, device), dst_ref=rows_of(into, me),
+                send_sem=send.at[k - 1], recv_sem=recv.at[me],
+                device_id={"seq": device}, device_id_type=MESH,
+            ).start()
+            return carry
+
+        lax.fori_loop(1, n, one, 0)
+        mine = pl.ds(pl.multiple_of(me * 8, 8), 8)
+        into[mine, :] = out[mine, :]
+
+    def collect(out, into, send, recv):
+        def one(k, carry):
+            source = (me + k) % n
+            copy = pltpu.make_async_remote_copy(
+                src_ref=rows_of(out, source), dst_ref=rows_of(into, source),
+                send_sem=send.at[k - 1], recv_sem=recv.at[source],
+                device_id={"seq": source}, device_id_type=MESH,
+            )
+            copy.wait_recv()
+            copy.wait_send()
+            return carry
+
+        lax.fori_loop(1, n, one, 0)
+        head_rows[pl.ds(0, n, stride=2), :] = into[pl.ds(0, n, stride=8), :]
+        head_rows[pl.ds(1, n, stride=2), :] = into[pl.ds(1, n, stride=8), :]
+
+    heads = x_ref.shape[0]
+
+    def project(every, weight):
+        wide[...] = every[...].astype(jnp.float32).reshape(n * heads, HD)
+        for k in range(heads):
+            lhs[:, k * HD:(k + 1) * HD] = wide[pl.ds(k, n, stride=heads), :].astype(jnp.bfloat16)
+        return jnp.dot(lhs[...], weight[...], preferred_element_type=jnp.float32)
+
+    norm_first, norm_second, norm_third, norm_last, norm_drain = gather(norm_own, norm_all, norm_send, norm_recv)
+    enc_first, enc_second, enc_third, enc_last, enc_drain = gather(enc_ref, enc_all, enc_send, enc_recv)
+    norm_first()
+    enc_first()
+    norm_second()
+    norm_third()
+    norm_last()
+    enc_second()
+    loads[0].wait()
+    scatter(project(norm_all, wq), q_out, q_in, q_send, q_recv)
+    enc_third()
+    enc_last()
+
+    tok_rows = enc_ref.shape[0]
+    group = 32 // tok_rows
+
+    def unpack(j, carry):
+        block = enc_all[pl.ds(j * group, group)].astype(jnp.float32)
+        enc_rows[pl.ds(pl.multiple_of(j * 32, 32), 32), :] = block.reshape(32, -1).astype(jnp.bfloat16)
+        return carry
+
+    lax.fori_loop(0, n // group, unpack, 0)
+
+    wide_a = EH * EHD
+
+    def own_tile(cols):
+        rows = enc_rows[:TILE_LEN, cols].astype(jnp.float32)
+        chosen = jnp.broadcast_to(tile_ref[...], rows.shape)
+        for t in range(1, enc_rows.shape[0] // TILE_LEN):
+            there = enc_rows[t * TILE_LEN:(t + 1) * TILE_LEN, cols].astype(jnp.float32)
+            rows = jnp.where(chosen == t, there, rows)
+        return rows
+
+    queries = own_tile(slice(0, wide_a)).astype(jnp.bfloat16)
+    lane = lax.broadcasted_iota(jnp.int32, (TILE_LEN, wide_a), 1)
+
+    def enc_head(h, acc):
+        inside = (lane >= h * EHD) & (lane < (h + 1) * EHD)
+        picked = jnp.where(inside, queries, jnp.zeros_like(queries))
+        scores = lax.dot_general(
+            picked, enc_rows[:, wide_a:2 * wide_a], (((1,), (1,)), ((), ())),
+            preferred_element_type=jnp.float32,
+        ) * EHD ** (-0.5)
+        powers = jnp.exp(scores - jnp.max(scores, axis=-1, keepdims=True))
+        weights = (powers / jnp.sum(powers, axis=-1, keepdims=True)).astype(jnp.bfloat16)
+        part = jnp.dot(weights, enc_rows[:, 2 * wide_a:3 * wide_a], preferred_element_type=jnp.float32)
+        return jnp.where(inside, part, acc)
+
+    enc_attn = lax.fori_loop(0, EH, enc_head, jnp.zeros((TILE_LEN, wide_a), jnp.float32)).astype(jnp.bfloat16)
+    loads[1].wait()
+    resid = own_tile(slice(3 * wide_a, enc_rows.shape[1])) + jnp.dot(
+        enc_attn, weo[...], preferred_element_type=jnp.float32
+    )
+    enc_feat[...] = layer_norm(resid).astype(jnp.bfloat16)
+    loads[2].wait()
+
+    def kv_columns(j, carry):
+        cols = pl.ds(pl.multiple_of(j * 256, 256), 256)
+        new_kv[:, cols] = jnp.dot(
+            enc_feat[...], wkv[:, cols], preferred_element_type=jnp.float32
+        ).astype(jnp.bfloat16)
+        return carry
+
+    lax.fori_loop(0, new_kv.shape[1] // 256, kv_columns, 0)
+
+    loads[3].wait()
+    collect(q_out, q_in, q_send, q_recv)
+    slots = cache.shape[0]
+    width = new_kv.shape[1] // 2
+    kv_heads = width // HD
+    each = heads // kv_heads
+    token = lax.broadcasted_iota(jnp.int32, (each, slots * TILE_LEN), 1)
+    cached = token // TILE_LEN < jnp.broadcast_to(count_ref[...], token.shape)
+    flip = (((1,), (1,)), ((), ()))
+    for g in range(kv_heads):
+        query = head_rows[g * each:(g + 1) * each, :].astype(jnp.bfloat16)
+        keys = slice(g * HD, (g + 1) * HD)
+        values = slice(width + g * HD, width + (g + 1) * HD)
+        old = lax.dot_general(
+            query, cache[:, :, keys].reshape(-1, HD), flip, preferred_element_type=jnp.float32
+        ) * HD ** (-0.5)
+        old = jnp.where(cached, old, -jnp.inf)
+        new = lax.dot_general(
+            query, new_kv[:, keys], flip, preferred_element_type=jnp.float32
+        ) * HD ** (-0.5)
+        top = jnp.maximum(jnp.max(old, axis=-1, keepdims=True), jnp.max(new, axis=-1, keepdims=True))
+        old = jnp.exp(old - top)
+        new = jnp.exp(new - top)
+        total = jnp.sum(old, axis=-1, keepdims=True) + jnp.sum(new, axis=-1, keepdims=True)
+        attn_heads[g * each:(g + 1) * each, :] = jnp.dot(
+            (old / total).astype(jnp.bfloat16), cache[:, :, values].reshape(-1, HD),
+            preferred_element_type=jnp.float32,
+        ) + jnp.dot(
+            (new / total).astype(jnp.bfloat16), new_kv[:, values], preferred_element_type=jnp.float32
+        )
+    dec_attn = attn_heads[...].astype(jnp.bfloat16)
+    attn_own[...] = dec_attn
+    attn_all[me] = dec_attn
+    attn_first, attn_second, attn_third, attn_last, attn_drain = gather(attn_own, attn_all, attn_send, attn_recv)
+    attn_first()
+    attn_second()
+    attn_third()
+    attn_last()
+    loads[4].wait()
+    scatter(project(attn_all, wo), o_out, o_in, o_send, o_recv)
+    norm_drain()
+    enc_drain()
+    attn_drain()
+    collect(o_out, o_in, o_send, o_recv)
+    out_ref[...] = (x_ref[...].astype(jnp.float32) + head_rows[...]).astype(jnp.bfloat16)
+
+
+def fused(n, enc_x, enc_qkv, w_eo, w_kv, dec_x, w_q, w_o, cache_kv, doc_tile, cached_count):
+    tok_rows = enc_x.shape[0]
+    packed = jnp.concatenate([enc_qkv.reshape(tok_rows, -1), enc_x], axis=1)
+    heads = dec_x.shape[1] // HD
+    tokens = n * tok_rows
+    bf16, f32 = jnp.bfloat16, jnp.float32
+    vmem = pl.BlockSpec(memory_space=pltpu.VMEM)
+    hbm = pl.BlockSpec(memory_space=pl.ANY)
+    dma = pltpu.SemaphoreType.DMA
+    piece = [pltpu.VMEM((heads, HD), bf16), pltpu.VMEM((n, heads, HD), bf16), dma((n,)), dma((n,))]
+    trade = [pltpu.VMEM((8 * n, HD), f32), pltpu.VMEM((8 * n, HD), f32), dma((n,)), dma((n,))]
+    out = pl.pallas_call(
+        functools.partial(fused_kernel, n),
+        out_shape=jax.ShapeDtypeStruct((heads, HD), bf16),
+        in_specs=[vmem, vmem, vmem, vmem, hbm, hbm, hbm, hbm, hbm],
+        out_specs=vmem,
+        scratch_shapes=[
+            pltpu.VMEM(w_eo.shape, bf16),
+            pltpu.VMEM(w_kv.shape, bf16),
+            pltpu.VMEM(w_q.shape, bf16),
+            pltpu.VMEM(w_o.shape, bf16),
+            pltpu.VMEM(cache_kv.shape[1:], bf16),
+            dma((5,)),
+            pltpu.VMEM((n,) + packed.shape, bf16),
+            dma((n,)),
+            dma((n,)),
+            pltpu.VMEM((tokens, packed.shape[1]), bf16),
+            pltpu.VMEM((TILE_LEN, enc_x.shape[1]), bf16),
+            pltpu.VMEM((TILE_LEN, w_kv.shape[1]), bf16),
+            *piece,
+            pltpu.VMEM((heads, HD), f32),
+            *piece,
+            pltpu.VMEM((n * heads, HD), f32),
+            pltpu.VMEM((n, heads * HD), bf16),
+            pltpu.VMEM((heads, HD), f32),
+            *trade,
+            *trade,
+        ],
+        compiler_params=pltpu.CompilerParams(collective_id=0, has_side_effects=True),
+    )(packed, dec_x.reshape(heads, HD), doc_tile.reshape(1, 1), cached_count.reshape(1, 1), w_eo, w_kv, w_q, w_o, cache_kv[0])
+    return out.reshape(1, -1)
+
+
 def solution(mesh):
+    n = mesh.shape["seq"]
     return jax.shard_map(
-        local,
+        functools.partial(fused, n) if n == 32 else local,
         mesh=mesh,
         in_specs=(
             P(("group", "seq"), None),

time: 227 us -> 62.1 us (0.27)
  blocking collectives: 171 us -> 0 us
  Pallas kernels: 0 us -> 56.2 us
  between operations: 15.5 us -> 1.31 us
  matrix products: 11.8 us -> 0 us
  local copies, waits for them, and re-layouts: 11.9 us -> 1.36 us
  waiting for transfers between devices: 5.86 us -> 0 us
  other arithmetic: 8.08 us -> 2.85 us
  starting transfers between devices: 2.46 us -> 0 us
    all_gather x4 -> x0, blocking collectives: 162 us -> none  [the longest x1 44.1 us: local(): key_piece = lax.all_gather(enc_qkv[:, 1], 'seq', axis=0, tiled=True)]
    pallas_call x0 -> x1, Pallas kernels: none -> 56.2 us  [fused(): pl.pallas_call(functools.partial(fused_kernel, n), out_shape=jax.ShapeDty...]
    dot_general x8 -> x0, matrix products: 11.8 us -> none  [the longest x1 3.93 us: local(): jnp.dot(features, w_kv, preferred_element_type=jnp.float32)]
    all_to_all x1 -> x0, blocking collectives: 8.87 us -> none  [local(): lax.all_to_all(output_cols, 'seq', split_axis=0, concat_axis=1, tiled=True)]
    all_to_all x1 -> x0, waiting for transfers between devices: 5.83 us -> none  [local(): lax.all_to_all(query_cols, 'seq', split_axis=0, concat_axis=1, tiled=True)]
    unnamed x16 -> x1, local copies, waits for them, and re-layouts: 6.99 us -> 1.36 us
    scatter-add x1 -> x0, other arithmetic: 4.8 us -> none  [local(): buffer.at[clipped]]
    slice x2 -> x0, local copies, waits for them, and re-layouts: 3.01 us -> none  [the longest x1 3 us: doc_attend(): key_heads = doc_kv[:, :width].reshape(length, kv_heads, HD)]
  transfers between devices with their start and end apart: 2 -> 0, of which waited for: 1 -> 0; matrix products, arithmetic and copies ran while one was open for 3% -> 0% of each run, Pallas kernels for 0% -> 0%
where the time goes in v1:
time: 62.1 us; the launch traced here: 61.8 us
  Pallas kernels  56.2 us (90%)
  other arithmetic  2.85 us (5%)
  local copies, waits for them, and re-layouts  1.36 us (2%)
  between operations  1.31 us (2%)
    pallas_call x1, Pallas kernels, fused(): pl.pallas_call(functools.partial(fused_kernel, n), out_shape=jax.ShapeDty...  56.2 us
    unnamed x1, other arithmetic  1.45 us
    concatenate x1, other arithmetic, fused(): packed = jnp.concatenate([enc_qkv.reshape(tok_rows, -1), enc_x], axis=1)  1.39 us
    unnamed x1, local copies, waits for them, and re-layouts  1.36 us

profile of v1, /device:TPU:0, one launch (start us, length us, event | category | flops | bytes accessed | tf_op | source)
XLA Modules:
  0.0 61.8 jit_solution(11194263846529708343)
XLA Ops:
  1.3 1.5 %reduce = bf16[8192]{0:T(1024)(128)(2,1)} reduce(bf16[1,8192]{1,0:T(2,128)(2,1)} %param.14, bf16[]{:T(256)} %constant.6), dimensions={0}, to_apply=%param.14.reduce_sub_computation | reduce | bytes 32770 | tf_op args[4]
  2.8 1.4 %pad_maximum_fusion.enc_ref = bf16[8,3200]{1,0:T(8,128)(2,1)} fusion(bf16[8,1280]{1,0:T(8,128)(2,1)} %param.10, bf16[8,1920]{1,0:T(8,128)(2,1)} %bitcast.15), kind=kLoop, calls=%fused_computation | loop fusion | flops 102400 | bytes 102400 | tf_op jit(solution)/shard_map/concatenate | solution.py:353
  4.1 56.2 %shard_map.100 = bf16[64,128]{1,0:T(8,128)(2,1)} custom-call(bf16[8,3200]{1,0:T(8,128)(2,1)} %pad_maximum_fusion.enc_ref, bf16[64,128]{1,0:T(8,128)(2,1)} %bitcast.13, s32[1,1]{1,0:T(1,128)} %bitcast.10.tile_ref, s32[1,1]{1,0:T(1,128)} %bitcast.11.count_ref, bf16[640,1280]{1,0:T(8,128)(2,1)} %weo_hbm.1, bf16[1280,2048]{1,0:T(8,128)(2,1)} %wkv_hbm.1, ...), custom_call_target="tpu_custom_call" | custom-call | tf_op jit(solution)/shard_map/pallas_call | solution.py:362
  60.4 1.4 %copy.13 = bf16[1,1,64,128]{3,1,2,0:T(2,128)(2,1)} copy(bf16[1,1,64,128]{3,2,1,0:T(8,128)(2,1)} %bitcast.14) | data formatting | bytes 32768

commit v2 on v1

--- a/solution.py
+++ b/solution.py
@@ -93,10 +93,10 @@
 
 
 def fused_kernel(
-    n, enc_ref, x_ref, tile_ref, count_ref, weo_hbm, wkv_hbm, wq_hbm, wo_hbm, cache_hbm, out_ref,
+    n, qkv_ref, resid_ref, x_ref, tile_ref, count_ref, weo_hbm, wkv_hbm, wq_hbm, wo_hbm, cache_hbm, out_ref,
     weo, wkv, wq, wo, cache, load_sem,
-    enc_all, enc_send, enc_recv, enc_rows, enc_feat, new_kv,
-    norm_own, norm_all, norm_send, norm_recv,
+    enc_own, enc_all, enc_send, enc_recv, enc_rows, enc_feat, new_kv,
+    x_rows, norm_own, norm_all, norm_send, norm_recv,
     attn_heads, attn_own, attn_all, attn_send, attn_recv,
     wide, lhs, head_rows,
     q_out, q_in, q_send, q_recv,
@@ -121,21 +121,24 @@
 
     barrier = pltpu.get_barrier_semaphore()
 
-    def greet(k, carry):
-        pl.semaphore_signal(barrier, inc=1, device_id={"seq": (me + k) % n}, device_id_type=MESH)
-        return carry
-
-    lax.fori_loop(1, n, greet, 0)
-
-    x_float = x_ref[...].astype(jnp.float32)
+    partners = [at(kz, 0, 0) for kz in range(1, outer)] + [at(0, kq, 0) for kq in range(1, inner)] + [at(0, 0, 1)]
+    for partner in partners:
+        pl.semaphore_signal(barrier, inc=1, device_id={"seq": partner}, device_id_type=MESH)
+
+    heads = x_rows.shape[0]
+    for k in range(heads):
+        x_rows[k:k + 1, :] = x_ref[:, k * HD:(k + 1) * HD].astype(jnp.float32)
+    x_float = x_rows[...]
     squares = jnp.sum(jnp.sum(x_float * x_float, axis=1, keepdims=True), axis=0, keepdims=True)
     normed = (x_float * lax.rsqrt(squares / x_float.size + 1e-05)).astype(jnp.bfloat16)
     norm_own[...] = normed
     norm_all[me] = normed
-    enc_all[me] = enc_ref[...]
-    q_out[...] = jnp.zeros_like(q_out)
-    o_out[...] = jnp.zeros_like(o_out)
-    pl.semaphore_wait(barrier, n - 1)
+    wide_a = EH * EHD
+    for j in range(3):
+        enc_own[:, j * wide_a:(j + 1) * wide_a] = qkv_ref[j]
+    enc_own[:, 3 * wide_a:] = resid_ref[...]
+    enc_all[me] = enc_own[...]
+    pl.semaphore_wait(barrier, len(partners))
 
     def gather(own, every, send, recv):
         def push(src, slot, sem, device):
@@ -191,32 +194,29 @@
 
         return first, second, third, last, drain
 
-    def rows_of(ref, index):
-        return ref.at[pl.ds(pl.multiple_of(index * 8, 8), 8), :]
-
     def scatter(values, out, into, send, recv):
         rounded = values.astype(jnp.bfloat16).astype(jnp.float32)
-        out[pl.ds(0, n, stride=8), :] = rounded[:, :HD]
-        out[pl.ds(1, n, stride=8), :] = rounded[:, HD:]
+        for d in range(n):
+            for half in range(2):
+                out[d, half:half + 1, :] = rounded[d:d + 1, half * HD:(half + 1) * HD]
 
         def one(k, carry):
             device = (me + k) % n
             pltpu.make_async_remote_copy(
-                src_ref=rows_of(out, device), dst_ref=rows_of(into, me),
+                src_ref=out.at[device], dst_ref=into.at[me],
                 send_sem=send.at[k - 1], recv_sem=recv.at[me],
                 device_id={"seq": device}, device_id_type=MESH,
             ).start()
             return carry
 
         lax.fori_loop(1, n, one, 0)
-        mine = pl.ds(pl.multiple_of(me * 8, 8), 8)
-        into[mine, :] = out[mine, :]
+        into[me] = out[me]
 
     def collect(out, into, send, recv):
         def one(k, carry):
             source = (me + k) % n
             copy = pltpu.make_async_remote_copy(
-                src_ref=rows_of(out, source), dst_ref=rows_of(into, source),
+                src_ref=out.at[source], dst_ref=into.at[source],
                 send_sem=send.at[k - 1], recv_sem=recv.at[source],
                 device_id={"seq": source}, device_id_type=MESH,
             )
@@ -225,10 +225,8 @@
             return carry
 
         lax.fori_loop(1, n, one, 0)
-        head_rows[pl.ds(0, n, stride=2), :] = into[pl.ds(0, n, stride=8), :]
-        head_rows[pl.ds(1, n, stride=2), :] = into[pl.ds(1, n, stride=8), :]
-
-    heads = x_ref.shape[0]
+        for d in range(n):
+            head_rows[2 * d:2 * d + 2, :] = into[d]
 
     def project(every, weight):
         wide[...] = every[...].astype(jnp.float32).reshape(n * heads, HD)
@@ -237,7 +235,7 @@
         return jnp.dot(lhs[...], weight[...], preferred_element_type=jnp.float32)
 
     norm_first, norm_second, norm_third, norm_last, norm_drain = gather(norm_own, norm_all, norm_send, norm_recv)
-    enc_first, enc_second, enc_third, enc_last, enc_drain = gather(enc_ref, enc_all, enc_send, enc_recv)
+    enc_first, enc_second, enc_third, enc_last, enc_drain = gather(enc_own, enc_all, enc_send, enc_recv)
     norm_first()
     enc_first()
     norm_second()
@@ -249,57 +247,63 @@
     enc_third()
     enc_last()
 
-    tok_rows = enc_ref.shape[0]
+    tok_rows = enc_own.shape[0]
     group = 32 // tok_rows
 
     def unpack(j, carry):
-        block = enc_all[pl.ds(j * group, group)].astype(jnp.float32)
+        block = enc_all[pl.ds(j * group, group), :, wide_a:3 * wide_a].astype(jnp.float32)
         enc_rows[pl.ds(pl.multiple_of(j * 32, 32), 32), :] = block.reshape(32, -1).astype(jnp.bfloat16)
         return carry
 
     lax.fori_loop(0, n // group, unpack, 0)
-
-    wide_a = EH * EHD
+    each_tile = TILE_LEN // tok_rows
 
     def own_tile(cols):
-        rows = enc_rows[:TILE_LEN, cols].astype(jnp.float32)
-        chosen = jnp.broadcast_to(tile_ref[...], rows.shape)
-        for t in range(1, enc_rows.shape[0] // TILE_LEN):
-            there = enc_rows[t * TILE_LEN:(t + 1) * TILE_LEN, cols].astype(jnp.float32)
-            rows = jnp.where(chosen == t, there, rows)
+        rows = None
+        for t in range(n // each_tile):
+            there = enc_all[t * each_tile:(t + 1) * each_tile, :, cols].astype(jnp.float32)
+            there = there.reshape(TILE_LEN, -1)
+            if rows is None:
+                rows, chosen = there, jnp.broadcast_to(tile_ref[...], there.shape)
+            else:
+                rows = jnp.where(chosen == t, there, rows)
         return rows
 
     queries = own_tile(slice(0, wide_a)).astype(jnp.bfloat16)
-    lane = lax.broadcasted_iota(jnp.int32, (TILE_LEN, wide_a), 1)
-
-    def enc_head(h, acc):
+    columns = [None] * (wide_a // HD)
+    for h in range(EH):
+        low, high = h * EHD // HD, (h * EHD + EHD - 1) // HD + 1
+        span = slice(low * HD, high * HD)
+        lane = lax.broadcasted_iota(jnp.int32, (TILE_LEN, (high - low) * HD), 1) + low * HD
         inside = (lane >= h * EHD) & (lane < (h + 1) * EHD)
-        picked = jnp.where(inside, queries, jnp.zeros_like(queries))
+        picked = jnp.where(inside, queries[:, span], jnp.zeros_like(queries[:, span]))
         scores = lax.dot_general(
-            picked, enc_rows[:, wide_a:2 * wide_a], (((1,), (1,)), ((), ())),
-            preferred_element_type=jnp.float32,
+            picked, enc_rows[:, span], (((1,), (1,)), ((), ())), preferred_element_type=jnp.float32
         ) * EHD ** (-0.5)
         powers = jnp.exp(scores - jnp.max(scores, axis=-1, keepdims=True))
         weights = (powers / jnp.sum(powers, axis=-1, keepdims=True)).astype(jnp.bfloat16)
-        part = jnp.dot(weights, enc_rows[:, 2 * wide_a:3 * wide_a], preferred_element_type=jnp.float32)
-        return jnp.where(inside, part, acc)
-
-    enc_attn = lax.fori_loop(0, EH, enc_head, jnp.zeros((TILE_LEN, wide_a), jnp.float32)).astype(jnp.bfloat16)
+        part = jnp.dot(
+            weights, enc_rows[:, wide_a + low * HD:wide_a + high * HD], preferred_element_type=jnp.float32
+        )
+        for b in range(low, high):
+            here = slice((b - low) * HD, (b - low + 1) * HD)
+            columns[b] = part[:, here] if columns[b] is None else jnp.where(inside[:, here], part[:, here], columns[b])
+    enc_attn = jnp.concatenate(columns, axis=1).astype(jnp.bfloat16)
     loads[1].wait()
-    resid = own_tile(slice(3 * wide_a, enc_rows.shape[1])) + jnp.dot(
+    resid = own_tile(slice(3 * wide_a, enc_own.shape[1])) + jnp.dot(
         enc_attn, weo[...], preferred_element_type=jnp.float32
     )
     enc_feat[...] = layer_norm(resid).astype(jnp.bfloat16)
     loads[2].wait()
 
     def kv_columns(j, carry):
-        cols = pl.ds(pl.multiple_of(j * 256, 256), 256)
+        cols = pl.ds(pl.multiple_of(j * 512, 512), 512)
         new_kv[:, cols] = jnp.dot(
             enc_feat[...], wkv[:, cols], preferred_element_type=jnp.float32
         ).astype(jnp.bfloat16)
         return carry
 
-    lax.fori_loop(0, new_kv.shape[1] // 256, kv_columns, 0)
+    lax.fori_loop(0, new_kv.shape[1] // 512, kv_columns, 0)
 
     loads[3].wait()
     collect(q_out, q_in, q_send, q_recv)
@@ -345,12 +349,12 @@
     enc_drain()
     attn_drain()
     collect(o_out, o_in, o_send, o_recv)
-    out_ref[...] = (x_ref[...].astype(jnp.float32) + head_rows[...]).astype(jnp.bfloat16)
+    out_ref[...] = (x_rows[...] + head_rows[...]).astype(jnp.bfloat16)
 
 
 def fused(n, enc_x, enc_qkv, w_eo, w_kv, dec_x, w_q, w_o, cache_kv, doc_tile, cached_count):
     tok_rows = enc_x.shape[0]
-    packed = jnp.concatenate([enc_qkv.reshape(tok_rows, -1), enc_x], axis=1)
+    packed = (tok_rows, enc_qkv.shape[1] * enc_qkv.shape[2] + enc_x.shape[1])
     heads = dec_x.shape[1] // HD
     tokens = n * tok_rows
     bf16, f32 = jnp.bfloat16, jnp.float32
@@ -358,11 +362,11 @@
     hbm = pl.BlockSpec(memory_space=pl.ANY)
     dma = pltpu.SemaphoreType.DMA
     piece = [pltpu.VMEM((heads, HD), bf16), pltpu.VMEM((n, heads, HD), bf16), dma((n,)), dma((n,))]
-    trade = [pltpu.VMEM((8 * n, HD), f32), pltpu.VMEM((8 * n, HD), f32), dma((n,)), dma((n,))]
+    trade = [pltpu.VMEM((n, 2, HD), f32), pltpu.VMEM((n, 2, HD), f32), dma((n,)), dma((n,))]
     out = pl.pallas_call(
         functools.partial(fused_kernel, n),
         out_shape=jax.ShapeDtypeStruct((heads, HD), bf16),
-        in_specs=[vmem, vmem, vmem, vmem, hbm, hbm, hbm, hbm, hbm],
+        in_specs=[vmem, vmem, vmem, vmem, vmem, hbm, hbm, hbm, hbm, hbm],
         out_specs=vmem,
         scratch_shapes=[
             pltpu.VMEM(w_eo.shape, bf16),
@@ -371,12 +375,14 @@
             pltpu.VMEM(w_o.shape, bf16),
             pltpu.VMEM(cache_kv.shape[1:], bf16),
             dma((5,)),
-            pltpu.VMEM((n,) + packed.shape, bf16),
+            pltpu.VMEM(packed, bf16),
+            pltpu.VMEM((n,) + packed, bf16),
             dma((n,)),
             dma((n,)),
-            pltpu.VMEM((tokens, packed.shape[1]), bf16),
+            pltpu.VMEM((tokens, 2 * enc_qkv.shape[2]), bf16),
             pltpu.VMEM((TILE_LEN, enc_x.shape[1]), bf16),
             pltpu.VMEM((TILE_LEN, w_kv.shape[1]), bf16),
+            pltpu.VMEM((heads, HD), f32),
             *piece,
             pltpu.VMEM((heads, HD), f32),
             *piece,
@@ -387,7 +393,7 @@
             *trade,
         ],
         compiler_params=pltpu.CompilerParams(collective_id=0, has_side_effects=True),
-    )(packed, dec_x.reshape(heads, HD), doc_tile.reshape(1, 1), cached_count.reshape(1, 1), w_eo, w_kv, w_q, w_o, cache_kv[0])
+    )(enc_qkv.transpose(1, 0, 2), enc_x, dec_x, doc_tile.reshape(1, 1), cached_count.reshape(1, 1), w_eo, w_kv, w_q, w_o, cache_kv[0])
     return out.reshape(1, -1)
 
 

time: 62.1 us -> 53.6 us (0.86)
  Pallas kernels: 56.2 us -> 50.7 us
  other arithmetic: 2.85 us -> 0 us
    pallas_call x1, Pallas kernels: 56.2 us -> 50.7 us  [fused(): pl.pallas_call(functools.partial(fused_kernel, n), out_shape=jax.ShapeDty...]
    unnamed x1 -> x0, other arithmetic: 1.45 us -> none
    concatenate x1 -> x0, other arithmetic: 1.39 us -> none  [fused(): packed = jnp.concatenate([enc_qkv.reshape(tok_rows, -1), enc_x], axis=1)]
where the time goes in v2:
time: 53.6 us; the launch traced here: 53.4 us
  Pallas kernels  50.7 us (95%)
  local copies, waits for them, and re-layouts  1.36 us (3%)
  between operations  1.3 us (2%)
    pallas_call x1, Pallas kernels, fused(): pl.pallas_call(functools.partial(fused_kernel, n), out_shape=jax.ShapeDty...  50.7 us
    unnamed x1, local copies, waits for them, and re-layouts  1.36 us

profile of v2, /device:TPU:0, one launch (start us, length us, event | category | flops | bytes accessed | tf_op | source)
XLA Modules:
  0.0 53.4 jit_solution(5143514593748636413)
XLA Ops:
  1.3 50.7 %shard_map.100 = bf16[64,128]{1,0:T(8,128)(2,1)} custom-call(bf16[3,8,640]{2,1,0:T(8,128)(2,1)} %bitcast.13, bf16[8,1280]{1,0:T(8,128)(2,1)} %resid_ref.1, bf16[1,8192]{1,0:T(2,128)(2,1)} %x_ref.1, s32[1,1]{1,0:T(1,128)} %bitcast.9.tile_ref, s32[1,1]{1,0:T(1,128)} %bitcast.10.count_ref, bf16[640,1280]{1,0:T(8,128)(2,1)} %weo_hbm.1, ...), custom_call_target="tpu_custom_call" | custom-call | tf_op jit(solution)/shard_map/pallas_call | solution.py:366
  52.0 1.4 %copy.13 = bf16[1,1,64,128]{3,1,2,0:T(2,128)(2,1)} copy(bf16[1,1,64,128]{3,2,1,0:T(8,128)(2,1)} %bitcast.12) | data formatting | bytes 32768

commit v3 on v2

--- a/solution.py
+++ b/solution.py
@@ -98,7 +98,7 @@
     enc_own, enc_all, enc_send, enc_recv, enc_rows, enc_feat, new_kv,
     x_rows, norm_own, norm_all, norm_send, norm_recv,
     attn_heads, attn_own, attn_all, attn_send, attn_recv,
-    wide, lhs, head_rows,
+    wide, lhs, head_rows, old_scores,
     q_out, q_in, q_send, q_recv,
     o_out, o_in, o_send, o_recv,
 ):
@@ -140,59 +140,76 @@
     enc_all[me] = enc_own[...]
     pl.semaphore_wait(barrier, len(partners))
 
-    def gather(own, every, send, recv):
-        def push(src, slot, sem, device):
+    flip_x = qi + 1 - 2 * (qi % 2)
+    flip_y = (qi + 2) % inner
+    flip_both = (flip_x + 2) % inner
+
+    def place(kz, plane, core):
+        return (zi + kz + outer) % outer * (2 * inner) + plane * 2 + core
+
+    def gather(own, every, send, recv, relay):
+        sent = [0]
+
+        def push(src, slot, device):
             pltpu.make_async_remote_copy(
-                src_ref=src, dst_ref=every.at[slot], send_sem=send.at[sem], recv_sem=recv.at[slot],
+                src_ref=src, dst_ref=every.at[slot], send_sem=send.at[sent[0]], recv_sem=recv.at[slot],
                 device_id={"seq": device}, device_id_type=MESH,
             ).start()
+            sent[0] += 1
 
         def take(slot):
             pltpu.make_async_remote_copy(
                 src_ref=own, dst_ref=every.at[slot], send_sem=send.at[0], recv_sem=recv.at[slot],
-                device_id={"seq": at(0, 0, 1)}, device_id_type=MESH,
+                device_id={"seq": place(0, qi, 1 - ci)}, device_id_type=MESH,
             ).wait_recv()
+
+        def spread(src, slot):
+            for plane in (flip_x, flip_y) if relay else (flip_both, flip_x, flip_y):
+                push(src, slot, place(0, plane, ci))
+            push(src, slot, place(0, qi, 1 - ci))
 
         def first():
             for kz in range(1, outer):
-                push(own, me, kz - 1, at(kz, 0, 0))
-            for kq in range(1, inner):
-                push(own, me, outer - 1 + kq - 1, at(0, kq, 0))
-            push(own, me, outer - 1 + inner - 1, at(0, 0, 1))
+                push(own, me, place(kz, qi, ci))
+            spread(own, me)
 
         def second():
             for kz in range(1, outer):
-                slot = at(-kz + outer, 0, 0)
+                slot = place(-kz, qi, ci)
                 take(slot)
-                base = outer - 1 + inner * kz
-                for kq in range(1, inner):
-                    push(every.at[slot], slot, base + kq - 1, at(0, kq, 0))
-                push(every.at[slot], slot, base + inner - 1, at(0, 0, 1))
+                spread(every.at[slot], slot)
 
         def third():
-            base = outer - 1 + inner * outer
             for kz in range(outer):
-                for kq in range(1, inner):
-                    slot = at(-kz + outer, -kq + inner, 0)
+                for odd, (plane, onward) in enumerate(((flip_x, flip_y), (flip_y, flip_x))):
+                    slot = place(-kz, plane, ci)
                     take(slot)
-                    push(every.at[slot], slot, base + kz * (inner - 1) + kq - 1, at(0, 0, 1))
+                    if relay and kz % 2 == odd:
+                        push(every.at[slot], slot, place(0, onward, ci))
+                    push(every.at[slot], slot, place(0, qi, 1 - ci))
+
+        def fourth():
+            for kz in range(outer):
+                slot = place(-kz, flip_both, ci)
+                take(slot)
+                push(every.at[slot], slot, place(0, qi, 1 - ci))
 
         def last():
-            for kz in range(outer):
-                for kq in range(inner):
-                    take(at(-kz + outer, -kq + inner, 1))
+            for plane in (qi, flip_x, flip_y, flip_both):
+                for kz in range(outer):
+                    take(place(-kz, plane, 1 - ci))
 
         def drain():
             def one(k, carry):
                 pltpu.make_async_remote_copy(
                     src_ref=own, dst_ref=every.at[0], send_sem=send.at[k], recv_sem=recv.at[0],
-                    device_id={"seq": at(0, 0, 1)}, device_id_type=MESH,
+                    device_id={"seq": place(0, qi, 1 - ci)}, device_id_type=MESH,
                 ).wait_send()
                 return carry
 
             lax.fori_loop(0, n - 1, one, 0)
 
-        return first, second, third, last, drain
+        return first, second, third, fourth, last, drain
 
     def scatter(values, out, into, send, recv):
         rounded = values.astype(jnp.bfloat16).astype(jnp.float32)
@@ -234,17 +251,34 @@
             lhs[:, k * HD:(k + 1) * HD] = wide[pl.ds(k, n, stride=heads), :].astype(jnp.bfloat16)
         return jnp.dot(lhs[...], weight[...], preferred_element_type=jnp.float32)
 
-    norm_first, norm_second, norm_third, norm_last, norm_drain = gather(norm_own, norm_all, norm_send, norm_recv)
-    enc_first, enc_second, enc_third, enc_last, enc_drain = gather(enc_own, enc_all, enc_send, enc_recv)
+    norm_first, norm_second, norm_third, norm_fourth, norm_last, norm_drain = gather(
+        norm_own, norm_all, norm_send, norm_recv, False
+    )
+    enc_first, enc_second, enc_third, enc_fourth, enc_last, enc_drain = gather(
+        enc_own, enc_all, enc_send, enc_recv, True
+    )
     norm_first()
     enc_first()
     norm_second()
+    enc_second()
     norm_third()
+    norm_fourth()
     norm_last()
-    enc_second()
     loads[0].wait()
     scatter(project(norm_all, wq), q_out, q_in, q_send, q_recv)
     enc_third()
+    enc_fourth()
+    loads[3].wait()
+    collect(q_out, q_in, q_send, q_recv)
+    width = new_kv.shape[1] // 2
+    kv_heads = width // HD
+    each = heads // kv_heads
+    flip = (((1,), (1,)), ((), ()))
+    for g in range(kv_heads):
+        old_scores[g * each:(g + 1) * each, :] = lax.dot_general(
+            head_rows[g * each:(g + 1) * each, :].astype(jnp.bfloat16),
+            cache[:, :, g * HD:(g + 1) * HD].reshape(-1, HD), flip, preferred_element_type=jnp.float32,
+        ) * HD ** (-0.5)
     enc_last()
 
     tok_rows = enc_own.shape[0]
@@ -305,23 +339,14 @@
 
     lax.fori_loop(0, new_kv.shape[1] // 512, kv_columns, 0)
 
-    loads[3].wait()
-    collect(q_out, q_in, q_send, q_recv)
     slots = cache.shape[0]
-    width = new_kv.shape[1] // 2
-    kv_heads = width // HD
-    each = heads // kv_heads
     token = lax.broadcasted_iota(jnp.int32, (each, slots * TILE_LEN), 1)
     cached = token // TILE_LEN < jnp.broadcast_to(count_ref[...], token.shape)
-    flip = (((1,), (1,)), ((), ()))
     for g in range(kv_heads):
         query = head_rows[g * each:(g + 1) * each, :].astype(jnp.bfloat16)
         keys = slice(g * HD, (g + 1) * HD)
         values = slice(width + g * HD, width + (g + 1) * HD)
-        old = lax.dot_general(
-            query, cache[:, :, keys].reshape(-1, HD), flip, preferred_element_type=jnp.float32
-        ) * HD ** (-0.5)
-        old = jnp.where(cached, old, -jnp.inf)
+        old = jnp.where(cached, old_scores[g * each:(g + 1) * each, :], -jnp.inf)
         new = lax.dot_general(
             query, new_kv[:, keys], flip, preferred_element_type=jnp.float32
         ) * HD ** (-0.5)
@@ -338,10 +363,13 @@
     dec_attn = attn_heads[...].astype(jnp.bfloat16)
     attn_own[...] = dec_attn
     attn_all[me] = dec_attn
-    attn_first, attn_second, attn_third, attn_last, attn_drain = gather(attn_own, attn_all, attn_send, attn_recv)
+    attn_first, attn_second, attn_third, attn_fourth, attn_last, attn_drain = gather(
+        attn_own, attn_all, attn_send, attn_recv, False
+    )
     attn_first()
     attn_second()
     attn_third()
+    attn_fourth()
     attn_last()
     loads[4].wait()
     scatter(project(attn_all, wo), o_out, o_in, o_send, o_recv)
@@ -389,6 +417,7 @@
             pltpu.VMEM((n * heads, HD), f32),
             pltpu.VMEM((n, heads * HD), bf16),
             pltpu.VMEM((heads, HD), f32),
+            pltpu.VMEM((heads, cache_kv.shape[1] * TILE_LEN), f32),
             *trade,
             *trade,
         ],

time: 53.6 us -> 50.3 us (0.938)
  Pallas kernels: 50.7 us -> 47.4 us
    pallas_call x1, Pallas kernels: 50.7 us -> 47.4 us  [fused(): pl.pallas_call(functools.partial(fused_kernel, n), out_shape=jax.ShapeDty...]
where the time goes in v3:
time: 50.3 us; the launch traced here: 50.1 us
  Pallas kernels  47.4 us (94%)
  local copies, waits for them, and re-layouts  1.36 us (3%)
  between operations  1.3 us (3%)
    pallas_call x1, Pallas kernels, fused(): pl.pallas_call(functools.partial(fused_kernel, n), out_shape=jax.ShapeDty...  47.4 us
    unnamed x1, local copies, waits for them, and re-layouts  1.36 us

profile of v3, /device:TPU:0, one launch (start us, length us, event | category | flops | bytes accessed | tf_op | source)
XLA Modules:
  0.0 50.1 jit_solution(17362160340330176865)
XLA Ops:
  1.3 47.4 %shard_map.100 = bf16[64,128]{1,0:T(8,128)(2,1)} custom-call(bf16[3,8,640]{2,1,0:T(8,128)(2,1)} %bitcast.13, bf16[8,1280]{1,0:T(8,128)(2,1)} %resid_ref.1, bf16[1,8192]{1,0:T(2,128)(2,1)} %x_ref.1, s32[1,1]{1,0:T(1,128)} %bitcast.9.tile_ref, s32[1,1]{1,0:T(1,128)} %bitcast.10.count_ref, bf16[640,1280]{1,0:T(8,128)(2,1)} %weo_hbm.1, ...), custom_call_target="tpu_custom_call" | custom-call | tf_op jit(solution)/shard_map/pallas_call | solution.py:394
  48.7 1.4 %copy.13 = bf16[1,1,64,128]{3,1,2,0:T(2,128)(2,1)} copy(bf16[1,1,64,128]{3,2,1,0:T(8,128)(2,1)} %bitcast.12) | data formatting | bytes 32768
